TPU v7x, 512 devices: a whole 4x4x16 slice. The times are simulated.
512 devices in a mesh: dp: 4 (over z_lo), row: 8 (over y, core), col: 16 (over z_hi, x).
Axes of the slice: x: 4, y: 4, z: 16 (z_hi: 4, z_lo: 4; z = z_hi * 4 + z_lo), core: 2. Of those that a mesh axis runs over, the one named last changes fastest.
Arguments:
- queries: bfloat16 [4, 64, 256, 768], P('dp', 'row', 'col'), may hold values from -5.5 to 5.5
- keys: bfloat16 [4, 64, 256, 768], P('dp', 'row', 'col'), may hold values from -5.5 to 5.5
- values: bfloat16 [4, 64, 256, 768], P('dp', 'row', 'col'), may hold values from -6 to 6
- occupancy: int32 [4, 8, 32], P('dp', 'row', 'col'), may hold values from 0 to 64, as said below
- out_weight: bfloat16 [768, 768], P('dp'), may hold values from -0.21875 to 0.21875
- grad_out: bfloat16 [4, 64, 256, 768], P('dp', 'row', 'col'), may hold values from -6 to 6
Outputs:
- grad_queries: bfloat16 [4, 64, 256, 768], P('dp', 'row', 'col')
- grad_keys: bfloat16 [4, 64, 256, 768], P('dp', 'row', 'col')
- grad_values: bfloat16 [4, 64, 256, 768], P('dp', 'row', 'col')
- grad_weight: float32 [768, 768], P('dp')
Inputs may be any that keep to these rules, and one draw needn't show every extreme that they name: `occupancy`: the occupied tiles of a block are its first that many tiles, row by row over its 8 x 8 tiles. Every slide has a block holding 8 * 8 and a block holding 0.
All inputs are finite; a program needn't handle non-finite values.
Results may differ from a plain program's by a relative error of at most 0.02.
Values may be sent and summed in bfloat16 or wider, within the bound.
A program may use at most 64 MiB of HBM per device.

v0:
```python
import jax
import jax.numpy as jnp
from jax import lax
from jax.sharding import PartitionSpec as P

HEAD_DIM = 64
SIDE = 8
REACH = 3
NEG = -1e30


def passed_along(value, axis, steps):
    count = lax.axis_size(axis)
    leading, last = (max(0, -steps), min(count, count - steps))
    return lax.ppermute(value, axis, [(source, source + steps) for source in range(leading, last)])


def for_sending(value):
    return jax.tree.map(lambda a: a.astype(jnp.bfloat16) if a.dtype == jnp.float32 else a, value)


def extended(cells, sides, width):
    for axis, dim in sides:
        count = lax.axis_size(axis)
        ends = count - 1
        head = lax.slice_in_dim(cells, 0, width, axis=dim)
        tail = lax.slice_in_dim(cells, cells.shape[dim] - width, cells.shape[dim], axis=dim)
        cells = jnp.concatenate(
            [
                lax.ppermute(tail, axis, [(i, (i + 1) % count) for i in range(ends)]),
                cells,
                lax.ppermute(head, axis, [((i + 1) % count, i) for i in range(ends)]),
            ],
            axis=dim,
        )
    return cells


def product(form, left, right):
    return jnp.einsum(form, left, right, preferred_element_type=jnp.float32)


def near_table(block_side, radius):
    window = block_side + 2 * radius
    queries_at = jnp.arange(block_side * block_side)
    keys_at = jnp.arange(window * window)
    row_gap = keys_at[None, :] // window - queries_at[:, None] // block_side - radius
    col_gap = keys_at[None, :] % window - queries_at[:, None] % block_side - radius
    return (jnp.abs(row_gap) <= radius) & (jnp.abs(col_gap) <= radius)


def tile_valid(counts, block_side):
    inside = jnp.arange(block_side * block_side, dtype=jnp.int32).reshape(block_side, block_side)
    flags = inside[None, :, None, :] < counts[:, None, :, None]
    return flags.reshape(counts.shape[0] * block_side, counts.shape[1] * block_side).astype(
        jnp.float32
    )


def blockify(source, block_side):
    height, breadth = (source.shape[0], source.shape[1])
    others = source.shape[2:]
    shaped = source.reshape(
        (height // block_side, block_side, breadth // block_side, block_side) + others
    )
    shaped = jnp.swapaxes(shaped, 1, 2)
    return shaped.reshape(
        (height // block_side, breadth // block_side, block_side * block_side) + others
    )


def unblock(source, block_side):
    block_rows, block_cols = (source.shape[0], source.shape[1])
    others = source.shape[3:]
    shaped = source.reshape((block_rows, block_cols, block_side, block_side) + others)
    shaped = jnp.swapaxes(shaped, 1, 2)
    return shaped.reshape((block_rows * block_side, block_cols * block_side) + others)


def cut_axis(source, dimension, block_side, radius, number):
    padding = [(0, 0)] * source.ndim
    padding[dimension] = (0, block_side - 2 * radius)
    shaped = jnp.pad(source, padding)
    shaped = shaped.reshape(
        source.shape[:dimension] + (number + 1, block_side) + source.shape[dimension + 1 :]
    )
    leading = lax.slice_in_dim(shaped, 0, number, axis=dimension)
    trailing = lax.slice_in_dim(
        lax.slice_in_dim(shaped, 1, number + 1, axis=dimension), 0, 2 * radius, axis=dimension + 1
    )
    return jnp.concatenate([leading, trailing], axis=dimension + 1)


def windows(source, block_side, radius, block_rows, block_cols):
    window = block_side + 2 * radius
    shaped = cut_axis(source, 0, block_side, radius, block_rows)
    shaped = cut_axis(shaped, 2, block_side, radius, block_cols)
    shaped = jnp.swapaxes(shaped, 1, 2)
    return shaped.reshape((block_rows * block_cols, window * window) + source.shape[2:])


def merge_axis(source, dimension, block_side, radius, number):
    leading = lax.slice_in_dim(source, 0, block_side, axis=dimension + 1)
    trailing = lax.slice_in_dim(source, block_side, block_side + 2 * radius, axis=dimension + 1)
    lead_pad = [(0, 0)] * source.ndim
    lead_pad[dimension] = (0, 1)
    trail_pad = [(0, 0)] * source.ndim
    trail_pad[dimension] = (1, 0)
    trail_pad[dimension + 1] = (0, block_side - 2 * radius)
    summed = jnp.pad(leading, lead_pad) + jnp.pad(trailing, trail_pad)
    summed = summed.reshape(
        source.shape[:dimension] + ((number + 1) * block_side,) + source.shape[dimension + 2 :]
    )
    return lax.slice_in_dim(summed, 0, number * block_side + 2 * radius, axis=dimension)


def fold_back(source, block_side, radius, block_rows, block_cols):
    window = block_side + 2 * radius
    shaped = source.reshape((block_rows, block_cols, window, window) + source.shape[2:])
    shaped = jnp.swapaxes(shaped, 1, 2)
    shaped = merge_axis(shaped, 2, block_side, radius, block_cols)
    return merge_axis(shaped, 0, block_side, radius, block_rows)


def attend(query_blocks, key_win, value_win, key_flag, query_flag, nearby, scaling):
    scores = product("nqhd,nkhd->nhqk", query_blocks, key_win) * scaling
    allowed = nearby[None, None] & (key_flag[:, None, None, :] > 0)
    masked = jnp.where(allowed, scores, NEG)
    highest = jnp.max(masked, axis=-1, keepdims=True)
    raised = jnp.exp(masked - highest)
    inverse = 1.0 / jnp.sum(raised, axis=-1, keepdims=True)
    weights = raised * inverse
    rounded = weights.astype(jnp.bfloat16)
    mixed = product("nhqk,nkhd->nqhd", rounded, value_win)
    attended = (mixed * query_flag[:, :, None, None]).astype(jnp.bfloat16)
    return (attended, weights, rounded, highest, inverse)


def query_side(weights, grad_blocks, key_win, value_win, scaling):
    prob_grad = product("nqhd,nkhd->nhqk", grad_blocks, value_win)
    correction = jnp.sum(weights * prob_grad, axis=-1, keepdims=True)
    score_grad = (weights * (prob_grad - correction) * scaling).astype(jnp.bfloat16)
    query_grad = product("nhqk,nkhd->nqhd", score_grad, key_win)
    return (query_grad, score_grad, correction)


def return_rims(key_full, value_full):
    middle = (key_full[REACH:-REACH], value_full[REACH:-REACH])
    for offset in (1, -1):
        if offset == 1:
            border = (key_full[-REACH:], value_full[-REACH:])
        else:
            border = (key_full[:REACH], value_full[:REACH])
        arrived = (
            passed_along(border[0].astype(jnp.bfloat16), "row", offset).astype(jnp.float32),
            passed_along(border[1].astype(jnp.bfloat16), "row", offset).astype(jnp.float32),
        )
        if offset == 1:
            middle = tuple(
                (portion.at[:REACH].add(incoming) for portion, incoming in zip(middle, arrived))
            )
        else:
            middle = tuple(
                (portion.at[-REACH:].add(incoming) for portion, incoming in zip(middle, arrived))
            )
    centre = tuple((portion[:, REACH:-REACH] for portion in middle))
    for offset in (1, -1):
        if offset == 1:
            border = tuple((portion[:, -REACH:] for portion in middle))
        else:
            border = tuple((portion[:, :REACH] for portion in middle))
        arrived = jax.tree.map(
            lambda part, own: part.astype(own.dtype),
            passed_along(for_sending(border), "col", offset),
            border,
        )
        if offset == 1:
            centre = tuple(
                (portion.at[:, :REACH].add(incoming) for portion, incoming in zip(centre, arrived))
            )
        else:
            centre = tuple(
                (portion.at[:, -REACH:].add(incoming) for portion, incoming in zip(centre, arrived))
            )
    return centre


def on_device(queries, keys, values, occupancy, out_weight, grad_out):
    query_tiles = queries[0]
    key_tiles = keys[0]
    value_tiles = values[0]
    grad_tiles = grad_out[0]
    counts = occupancy[0]
    height, breadth, channels = query_tiles.shape
    out_width = grad_tiles.shape[2]
    head_count = channels // HEAD_DIM
    block_rows = height // SIDE
    block_cols = breadth // SIDE
    block_count = block_rows * block_cols
    block_area = SIDE * SIDE
    window = SIDE + 2 * REACH
    window_area = window * window
    tile_count = height * breadth
    nearby = near_table(SIDE, REACH)
    scaling = HEAD_DIM ** (-0.5)
    occupied = tile_valid(counts, SIDE)
    key_ext, value_ext, flag_ext = (
        extended(key_tiles, (("row", 0), ("col", 1)), REACH),
        extended(value_tiles, (("row", 0), ("col", 1)), REACH),
        extended(occupied.astype(jnp.bfloat16), (("row", 0), ("col", 1)), REACH),
    )
    key_win = windows(key_ext, SIDE, REACH, block_rows, block_cols).reshape(
        block_count, window_area, head_count, HEAD_DIM
    )
    value_win = windows(value_ext, SIDE, REACH, block_rows, block_cols).reshape(
        block_count, window_area, head_count, HEAD_DIM
    )
    flag_win = windows(flag_ext, SIDE, REACH, block_rows, block_cols)
    query_blocks = blockify(query_tiles, SIDE).reshape(
        block_count, block_area, head_count, HEAD_DIM
    )
    query_flag = blockify(occupied, SIDE).reshape(block_count, block_area)
    attended, weights, rounded, highest, inverse = attend(
        query_blocks, key_win, value_win, flag_win, query_flag, nearby, scaling
    )
    flat_grads = grad_tiles.reshape(tile_count, out_width)
    out_back = lax.dot_general(
        flat_grads,
        lax.all_gather(out_weight, "dp", axis=0, tiled=True),
        (((1,), (1,)), ((), ())),
        preferred_element_type=jnp.float32,
    )
    gated_grad = out_back.astype(jnp.bfloat16).reshape(height, breadth, channels) * occupied[
        :, :, None
    ].astype(jnp.bfloat16)
    grad_blocks = blockify(gated_grad, SIDE).reshape(block_count, block_area, head_count, HEAD_DIM)
    out_blocks = blockify(grad_tiles, SIDE).reshape(tile_count, out_width)
    weight_term = lax.dot_general(
        attended.reshape(tile_count, channels),
        out_blocks,
        (((0,), (0,)), ((), ())),
        preferred_element_type=jnp.float32,
    )
    summed = lax.psum(weight_term, ("row", "col"))
    slide_part = lax.psum_scatter(
        summed.astype(jnp.bfloat16), "dp", scatter_dimension=0, tiled=True
    ).astype(jnp.float32)
    all_tiles = tile_count * lax.axis_size("dp") * lax.axis_size("row") * lax.axis_size("col")
    grad_weight = slide_part * all_tiles ** (-0.5)
    query_grad, score_grad, correction = query_side(
        weights, grad_blocks, key_win, value_win, scaling
    )
    key_part = product("nhqk,nqhd->nkhd", score_grad, query_blocks).reshape(
        block_count, window_area, channels
    )
    value_part = product("nhqk,nqhd->nkhd", rounded, grad_blocks).reshape(
        block_count, window_area, channels
    )
    key_full = fold_back(key_part, SIDE, REACH, block_rows, block_cols)
    value_full = fold_back(value_part, SIDE, REACH, block_rows, block_cols)
    key_sum, value_sum = return_rims(key_full, value_full)
    grad_query = unblock(query_grad.reshape(block_rows, block_cols, block_area, channels), SIDE)
    return (
        grad_query.astype(jnp.bfloat16)[None],
        key_sum.astype(jnp.bfloat16)[None],
        value_sum.astype(jnp.bfloat16)[None],
        grad_weight,
    )


def solution(mesh):
    return jax.shard_map(
        on_device,
        mesh=mesh,
        in_specs=(
            P("dp", "row", "col", None),
            P("dp", "row", "col", None),
            P("dp", "row", "col", None),
            P("dp", "row", "col"),
            P("dp", None),
            P("dp", "row", "col", None),
        ),
        out_specs=(
            P("dp", "row", "col", None),
            P("dp", "row", "col", None),
            P("dp", "row", "col", None),
            P("dp", None),
        ),
        check_vma=False,
    )
```

profile of v0, /device:TPU:39, one launch (start us, length us, event | category | flops | bytes accessed | tf_op | source)
XLA Modules:
  0.0 1018.1 jit_solution(9643661524782293680)
XLA Ops:
  8.3 2.6 collective-permute-start.1
  10.9 3.1 collective-permute-start
  19.8 3.6 collective-permute-start.4
  27.3 2.4 collective-permute-start.7
  29.7 8.8 collective-permute-start.6
  38.6 3.0 collective-permute-start.8
  44.1 9.4 collective-permute-start.2
  55.6 9.4 collective-permute-start.10
  66.7 9.1 collective-permute-done.11
  80.4 2.4 fusion.67
  88.0 4.9 fusion.24
  95.6 764.2 %all-reduce.15 = bf16[768,768]{1,0:T(8,128)(2,1)} all-reduce(f32[768,768]{1,0:T(8,128)S(1)} %fusion.69), channel_id=1, replica_groups=mesh['dp'=4,'row'=8,'col'=16] {'row','col'}, use_global_device_ids=true, to_apply=%region_3.4 | all-reduce | flops 589824 | bytes 3538944 | tf_op jit(solution)/shard_map/psum | solution.py:244
  864.2 11.5 %fusion.25 = bf16[2,64,12,64]{1,3,2,0:T(8,128)(2,1)} fusion(bf16[2,196,12,64]{1,3,2,0:T(8,128)(2,1)S(1)} %copy.80, f32[2,12,64,196]{3,2,1,0:T(8,128)} %fusion.68, f32[2,12,64,196]{3,2,1,0:T(8,128)} %get-tuple-element.127, f32[2,12,64]{2,1,0:T(8,128)S(1)} %broadcast_divide_fusion), kind=kOutput, calls=%fused_computation.21 | convolution fusion | flops 40742596 | bytes 3213312 | tf_op jit(solution)/shard_map/nhqk,nkhd->nqhd/dot_general | solution.py:40
  875.7 11.9 %fusion.12 = f32[2,196,12,64]{1,3,2,0:T(8,128)} fusion(bf16[2,64,12,64]{1,3,2,0:T(8,128)(2,1)S(1)} %copy-done.10, f32[2,12,64,196]{3,2,1,0:T(8,128)} %fusion.68, f32[2,12,64,196]{3,2,1,0:T(8,128)} %get-tuple-element.127, f32[2,12,64]{2,1,0:T(8,128)S(1)} %broadcast_divide_fusion), kind=kOutput, calls=%fused_computation.9 | convolution fusion | flops 40644292 | bytes 3815424 | tf_op jit(solution)/shard_map/nhqk,nqhd->nkhd/dot_general | solution.py:40
  887.7 3.5 copy.84
  897.9 5.8 convolution_bitcast_fusion
  903.7 3.5 copy.87
  917.1 51.0 %collective-permute-start.13 = (bf16[3,22,768]{2,1,0:T(8,128)(2,1)S(1)}, bf16[3,22,768]{2,1,0:T(8,128)(2,1)S(1)}, u32[]{:S(2)}, u32[]{:S(2)}) collective-permute-start(bf16[3,22,768]{2,1,0:T(8,128)(2,1)S(1)} %get-tuple-element.102), channel_id=1, source_target_pairs={{16,0},{32,16},{48,32},{64,48},{80,64},{96,80},{112,96},{17,1},{33... | collective-permute-start | bytes 304136 | tf_op jit(solution)/shard_map/ppermute | solution.py:15
  970.0 2.4 collective-permute-start.17
  972.7 3.4 collective-permute-done.17
  976.3 9.0 collective-permute-start.14
  985.3 3.1 collective-permute-start.15
  988.5 8.2 collective-permute-start.18
  999.8 7.9 collective-permute-done.19
  (182 shorter events, 58.9 us)
Async XLA Ops:
  7.2 852.7 %all-gather.2.cloned.1.call-start = ((), (), s32[]{:S(2)}) async-start(), calls=%async_computation.1 | async-start | bytes 1474560 | tf_op jit(solution)/shard_map/all_gather | solution.py:229
  8.3 33.8 %collective-permute-start.1 = (bf16[3,16,768]{2,1,0:T(8,128)(2,1)S(1)}, bf16[3,16,768]{2,1,0:T(8,128)(2,1)S(1)}, u32[]{:S(2)}, u32[]{:S(2)}) collective-permute-start(bf16[3,16,768]{2,1,0:T(8,128)(2,1)S(1)} %get-tuple-element.119), channel_id=1, source_target_pairs={{16,0},{32,16},{48,32},{64,48},{80,64},{96,80},{112,96},{17,1},{33... | collective-permute-start | bytes 221192 | tf_op jit(solution)/shard_map/ppermute | solution.py:32
  10.9 31.2 %collective-permute-start = (bf16[3,16,768]{2,1,0:T(8,128)(2,1)S(1)}, bf16[3,16,768]{2,1,0:T(8,128)(2,1)S(1)}, u32[]{:S(2)}, u32[]{:S(2)}) collective-permute-start(bf16[3,16,768]{2,1,0:T(8,128)(2,1)S(1)} %get-tuple-element.118), channel_id=1, source_target_pairs={{0,16},{16,32},{32,48},{48,64},{64,80},{80,96},{96,112},{1,17},{17... | collective-permute-start | bytes 221192 | tf_op jit(solution)/shard_map/ppermute | solution.py:30
  14.0 995.5 %reduce-scatter.2.cloned.1.call-start = ((), (), s32[]{:S(2)}) async-start(), calls=%async_computation.2 | async-start | bytes 1474560 | tf_op jit(solution)/shard_map/reduce_scatter | solution.py:245
  15.0 38.5 %collective-permute-start.9 = (bf16[3,16,768]{2,1,0:T(8,128)(2,1)S(1)}, bf16[3,16,768]{2,1,0:T(8,128)(2,1)S(1)}, u32[]{:S(2)}, u32[]{:S(2)}) collective-permute-start(bf16[3,16,768]{2,1,0:T(8,128)(2,1)S(1)} %get-tuple-element.117), channel_id=1, source_target_pairs={{16,0},{32,16},{48,32},{64,48},{80,64},{96,80},{112,96},{17,1},{33... | collective-permute-start | bytes 221192 | tf_op jit(solution)/shard_map/ppermute | solution.py:32
  17.9 9.3 collective-permute-start.5
  19.8 7.4 collective-permute-start.4
  26.3 56.6 %copy-start.9 = (bf16[2,64,12,64]{1,3,2,0:T(8,128)(2,1)}, bf16[2,64,12,64]{1,3,2,0:T(8,128)(2,1)S(1)}, u32[]{:S(2)}) copy-start(bf16[2,64,12,64]{1,3,2,0:T(8,128)(2,1)S(1)} %copy.83) | copy-start | bytes 589828
  27.3 11.3 %collective-permute-start.7 = (bf16[14,3]{1,0:T(8,128)(2,1)S(1)}, bf16[14,3]{1,0:T(8,128)(2,1)S(1)}, u32[]{:S(2)}, u32[]{:S(2)}) collective-permute-start(bf16[14,3]{1,0:T(8,128)(2,1)S(1)} %get-tuple-element.123), channel_id=1, source_target_pairs={{1,0},{2,1},{3,2},{4,3},{5,4},{6,5},{7,6},{8,7},{9,8},{10,9},{11,1... | collective-permute-start | bytes 260 | tf_op jit(solution)/shard_map/ppermute | solution.py:32
  29.7 11.8 %collective-permute-start.6 = (bf16[14,3]{1,0:T(8,128)(2,1)S(1)}, bf16[14,3]{1,0:T(8,128)(2,1)S(1)}, u32[]{:S(2)}, u32[]{:S(2)}) collective-permute-start(bf16[14,3]{1,0:T(8,128)(2,1)S(1)} %get-tuple-element.122), channel_id=1, source_target_pairs={{0,1},{1,2},{2,3},{3,4},{4,5},{5,6},{6,7},{7,8},{8,9},{9,10},{10,1... | collective-permute-start | bytes 260 | tf_op jit(solution)/shard_map/ppermute | solution.py:30
  38.6 14.9 %collective-permute-start.8 = (bf16[3,16,768]{2,1,0:T(8,128)(2,1)S(1)}, bf16[3,16,768]{2,1,0:T(8,128)(2,1)S(1)}, u32[]{:S(2)}, u32[]{:S(2)}) collective-permute-start(bf16[3,16,768]{2,1,0:T(8,128)(2,1)S(1)} %get-tuple-element.116), channel_id=1, source_target_pairs={{0,16},{16,32},{32,48},{48,64},{64,80},{80,96},{96,112},{1,17},{17... | collective-permute-start | bytes 221192 | tf_op jit(solution)/shard_map/ppermute | solution.py:30
  42.2 24.1 %collective-permute-start.3 = (bf16[14,3,768]{2,1,0:T(4,128)(2,1)S(1)}, bf16[14,3,768]{2,1,0:T(4,128)(2,1)S(1)}, u32[]{:S(2)}, u32[]{:S(2)}) collective-permute-start(bf16[14,3,768]{2,1,0:T(4,128)(2,1)S(1)} %get-tuple-element.111), channel_id=1, source_target_pairs={{1,0},{2,1},{3,2},{4,3},{5,4},{6,5},{7,6},{8,7},{9,8},{10,9},{11,1... | collective-permute-start | bytes 193544 | tf_op jit(solution)/shard_map/ppermute | solution.py:32
  44.1 22.2 %collective-permute-start.2 = (bf16[14,3,768]{2,1,0:T(4,128)(2,1)S(1)}, bf16[14,3,768]{2,1,0:T(4,128)(2,1)S(1)}, u32[]{:S(2)}, u32[]{:S(2)}) collective-permute-start(bf16[14,3,768]{2,1,0:T(4,128)(2,1)S(1)} %get-tuple-element.110), channel_id=1, source_target_pairs={{0,1},{1,2},{2,3},{3,4},{4,5},{5,6},{6,7},{7,8},{8,9},{9,10},{10,1... | collective-permute-start | bytes 193544 | tf_op jit(solution)/shard_map/ppermute | solution.py:30
  53.6 22.2 %collective-permute-start.11 = (bf16[14,3,768]{2,1,0:T(4,128)(2,1)S(1)}, bf16[14,3,768]{2,1,0:T(4,128)(2,1)S(1)}, u32[]{:S(2)}, u32[]{:S(2)}) collective-permute-start(bf16[14,3,768]{2,1,0:T(4,128)(2,1)S(1)} %get-tuple-element.109), channel_id=1, source_target_pairs={{1,0},{2,1},{3,2},{4,3},{5,4},{6,5},{7,6},{8,7},{9,8},{10,9},{11,1... | collective-permute-start | bytes 193544 | tf_op jit(solution)/shard_map/ppermute | solution.py:32
  55.6 20.3 %collective-permute-start.10 = (bf16[14,3,768]{2,1,0:T(4,128)(2,1)S(1)}, bf16[14,3,768]{2,1,0:T(4,128)(2,1)S(1)}, u32[]{:S(2)}, u32[]{:S(2)}) collective-permute-start(bf16[14,3,768]{2,1,0:T(4,128)(2,1)S(1)} %get-tuple-element.108), channel_id=1, source_target_pairs={{0,1},{1,2},{2,3},{3,4},{4,5},{5,6},{6,7},{7,8},{8,9},{9,10},{10,1... | collective-permute-start | bytes 193544 | tf_op jit(solution)/shard_map/ppermute | solution.py:30
  95.6 764.3 %copy-start.15 = (bf16[1,8,16,768]{3,2,1,0:T(8,128)(2,1)S(1)}, bf16[1,8,16,768]{3,2,1,0:T(8,128)(2,1)}, u32[]{:S(2)}) copy-start(bf16[1,8,16,768]{3,2,1,0:T(8,128)(2,1)} %param.27) | copy-start | bytes 589828
  914.9 57.5 %collective-permute-start.12 = (bf16[3,22,768]{2,1,0:T(8,128)(2,1)S(1)}, bf16[3,22,768]{2,1,0:T(8,128)(2,1)S(1)}, u32[]{:S(2)}, u32[]{:S(2)}) collective-permute-start(bf16[3,22,768]{2,1,0:T(8,128)(2,1)S(1)} %get-tuple-element.103), channel_id=1, source_target_pairs={{0,16},{16,32},{32,48},{48,64},{64,80},{80,96},{96,112},{1,17},{17... | collective-permute-start | bytes 304136 | tf_op jit(solution)/shard_map/ppermute | solution.py:15
  917.1 55.4 %collective-permute-start.13 = (bf16[3,22,768]{2,1,0:T(8,128)(2,1)S(1)}, bf16[3,22,768]{2,1,0:T(8,128)(2,1)S(1)}, u32[]{:S(2)}, u32[]{:S(2)}) collective-permute-start(bf16[3,22,768]{2,1,0:T(8,128)(2,1)S(1)} %get-tuple-element.102), channel_id=1, source_target_pairs={{16,0},{32,16},{48,32},{64,48},{80,64},{96,80},{112,96},{17,1},{33... | collective-permute-start | bytes 304136 | tf_op jit(solution)/shard_map/ppermute | solution.py:15
  968.1 4.4 collective-permute-start.16
  970.0 6.1 collective-permute-start.17
  976.3 22.3 %collective-permute-start.14 = (bf16[8,3,768]{2,1,0:T(4,128)(2,1)S(1)}, bf16[8,3,768]{2,1,0:T(4,128)(2,1)S(1)}, u32[]{:S(2)}, u32[]{:S(2)}) collective-permute-start(bf16[8,3,768]{2,1,0:T(4,128)(2,1)S(1)} %get-tuple-element.115), channel_id=1, source_target_pairs={{0,1},{1,2},{2,3},{3,4},{4,5},{5,6},{6,7},{7,8},{8,9},{9,10},{10,1... | collective-permute-start | bytes 110600 | tf_op jit(solution)/shard_map/ppermute | solution.py:15
  985.3 13.8 %collective-permute-start.15 = (bf16[8,3,768]{2,1,0:T(4,128)(2,1)S(1)}, bf16[8,3,768]{2,1,0:T(4,128)(2,1)S(1)}, u32[]{:S(2)}, u32[]{:S(2)}) collective-permute-start(bf16[8,3,768]{2,1,0:T(4,128)(2,1)S(1)} %get-tuple-element.114), channel_id=1, source_target_pairs={{1,0},{2,1},{3,2},{4,3},{5,4},{6,5},{7,6},{8,7},{9,8},{10,9},{11,1... | collective-permute-start | bytes 110600 | tf_op jit(solution)/shard_map/ppermute | solution.py:15
  988.5 10.2 collective-permute-start.18
  996.7 11.1 %collective-permute-start.19 = (bf16[8,3,768]{2,1,0:T(4,128)(2,1)S(1)}, bf16[8,3,768]{2,1,0:T(4,128)(2,1)S(1)}, u32[]{:S(2)}, u32[]{:S(2)}) collective-permute-start(bf16[8,3,768]{2,1,0:T(4,128)(2,1)S(1)} %get-tuple-element.112), channel_id=1, source_target_pairs={{1,0},{2,1},{3,2},{4,3},{5,4},{6,5},{7,6},{8,7},{9,8},{10,9},{11,1... | collective-permute-start | bytes 110600 | tf_op jit(solution)/shard_map/ppermute | solution.py:15
  (19 other events, 153.0 us)
Sparse Core Ops, SparseCore 0:
  14.1 41.7 all-gather.1
  860.0 89.8 reduce-scatter.1
where the time goes:
time: 1020 us
  blocking collectives  764 us (75%)
  starting transfers between devices  130 us (13%)
  matrix products  43 us (4%)
  local copies, waits for them, and re-layouts  35 us (3%)
  waiting for transfers between devices  21.9 us (2%)
  between operations  15.1 us (1%)
    psum x1, blocking collectives, on_device(): summed = lax.psum(weight_term, ('row', 'col'))  764 us
    ppermute x8, starting transfers between devices, passed_along(): lax.ppermute(value, axis, [(source, source + steps) for source in range(l...  79.4 us
    ppermute x6, starting transfers between devices, extended(): lax.ppermute(tail, axis, [(i, (i + 1) % count) for i in range(ends)])  37.3 us
    dot_general x6, matrix products, product(): return jnp.einsum(form, left, right, preferred_element_type=jnp.float32)  37.2 us
  transfers between devices with their start and end apart: 22, of which 4 were waited for; matrix products, arithmetic and copies ran while one was open for 8% of the time, Pallas kernels for 0%

commit v1 on v0

--- a/solution.py
+++ b/solution.py
@@ -1,3 +1,4 @@
+import functools
 import jax
 import jax.numpy as jnp
 from jax import lax
@@ -7,6 +8,14 @@
 SIDE = 8
 REACH = 3
 NEG = -1e30
+
+
+def spread_the_screen(local, mesh_ax, bus_axis):
+    item_now = lax.psum(lax.psum(local, mesh_ax), bus_axis)
+    return item_now
+
+
+make_map = functools.partial(spread_the_screen, mesh_ax="row", bus_axis="col")
 
 
 def passed_along(value, axis, steps):
@@ -241,7 +250,7 @@
         (((0,), (0,)), ((), ())),
         preferred_element_type=jnp.float32,
     )
-    summed = lax.psum(weight_term, ("row", "col"))
+    summed = make_map(weight_term)
     slide_part = lax.psum_scatter(
         summed.astype(jnp.bfloat16), "dp", scatter_dimension=0, tiled=True
     ).astype(jnp.float32)

time: 1020 us -> 518 us (0.51)
  the two profiles are of different devices: /device:TPU:39 before, /device:TPU:47 now
where the time goes in v1:
time: 518 us; the launch traced here: 517 us
  blocking collectives  222 us (43%)
  waiting for transfers between devices  102 us (20%)
  starting transfers between devices  91 us (18%)
  matrix products  42.6 us (8%)
  local copies, waits for them, and re-layouts  34.3 us (7%)
  between operations  16.5 us (3%)
  other arithmetic  8.16 us (2%)
    psum x1, blocking collectives, spread_the_screen(): item_now = lax.psum(lax.psum(local, mesh_ax), bus_axis)  222 us
    psum x1, waiting for transfers between devices, spread_the_screen(): item_now = lax.psum(lax.psum(local, mesh_ax), bus_axis)  83.4 us
    ppermute x8, starting transfers between devices, passed_along(): lax.ppermute(value, axis, [(source, source + steps) for source in range(l...  40.7 us
    dot_general x6, matrix products, product(): return jnp.einsum(form, left, right, preferred_element_type=jnp.float32)  37.1 us
    ppermute x6, starting transfers between devices, extended(): lax.ppermute(tail, axis, [(i, (i + 1) % count) for i in range(ends)])  36.8 us
    ppermute x6, starting transfers between devices, extended(): lax.ppermute(head, axis, [((i + 1) % count, i) for i in range(ends)])  13.4 us
    ppermute x8, waiting for transfers between devices, passed_along(): lax.ppermute(value, axis, [(source, source + steps) for source in range(l...  11.9 us
  transfers between devices with their start and end apart: 23, of which 4 were waited for; matrix products, arithmetic and copies ran while one was open for 12% of the time, Pallas kernels for 0%

profile of v1, /device:TPU:47, one launch (start us, length us, event | category | flops | bytes accessed | tf_op | source)
XLA Modules:
  0.0 516.9 jit_solution(2992925853900233234)
XLA Ops:
  9.1 2.7 collective-permute-start.1
  11.8 3.1 collective-permute-start
  18.7 2.5 collective-permute-start.5
  21.2 3.1 collective-permute-start.4
  26.8 2.4 collective-permute-start.7
  29.3 8.8 %collective-permute-start.6 = (bf16[14,3]{1,0:T(8,128)(2,1)S(1)}, bf16[14,3]{1,0:T(8,128)(2,1)S(1)}, u32[]{:S(2)}, u32[]{:S(2)}) collective-permute-start(bf16[14,3]{1,0:T(8,128)(2,1)S(1)} %get-tuple-element.122), channel_id=1, source_target_pairs={{0,1},{1,2},{2,3},{3,4},{4,5},{5,6},{6,7},{7,8},{8,9},{9,10},{10,1... | collective-permute-start | bytes 260 | tf_op jit(solution)/shard_map/ppermute | solution.py:39
  38.2 3.0 collective-permute-start.8
  43.7 9.4 %collective-permute-start.2 = (bf16[14,3,768]{2,1,0:T(4,128)(2,1)S(1)}, bf16[14,3,768]{2,1,0:T(4,128)(2,1)S(1)}, u32[]{:S(2)}, u32[]{:S(2)}) collective-permute-start(bf16[14,3,768]{2,1,0:T(4,128)(2,1)S(1)} %get-tuple-element.110), channel_id=1, source_target_pairs={{0,1},{1,2},{2,3},{3,4},{4,5},{5,6},{6,7},{7,8},{8,9},{9,10},{10,1... | collective-permute-start | bytes 193544 | tf_op jit(solution)/shard_map/ppermute | solution.py:39
  55.2 9.4 %collective-permute-start.10 = (bf16[14,3,768]{2,1,0:T(4,128)(2,1)S(1)}, bf16[14,3,768]{2,1,0:T(4,128)(2,1)S(1)}, u32[]{:S(2)}, u32[]{:S(2)}) collective-permute-start(bf16[14,3,768]{2,1,0:T(4,128)(2,1)S(1)} %get-tuple-element.108), channel_id=1, source_target_pairs={{0,1},{1,2},{2,3},{3,4},{4,5},{5,6},{6,7},{7,8},{8,9},{9,10},{10,1... | collective-permute-start | bytes 193544 | tf_op jit(solution)/shard_map/ppermute | solution.py:39
  65.0 6.2 %collective-permute-done.11 = bf16[14,3,768]{2,1,0:T(4,128)(2,1)S(1)} collective-permute-done((bf16[14,3,768]{2,1,0:T(4,128)(2,1)S(1)}, bf16[14,3,768]{2,1,0:T(4,128)(2,1)S(1)}, u32[]{:S(2)}, u32[]{:S(2)}) %collective-permute-start.11) | collective-permute-done | bytes 64544 | tf_op jit(solution)/shard_map/ppermute | solution.py:41
  82.8 4.7 fusion.24
  90.7 83.4 %all-reduce.17.cloned.1.call-done = f32[768,768]{1,0:T(8,128)} async-done(((f32[768,768]{1,0:T(8,128)}), f32[768,768]{1,0:T(8,128)}) %all-reduce.17.cloned.1.call-update) | async-done | bytes 2359312 | tf_op jit(solution)/shard_map/psum | solution.py:14
  174.1 222.2 %all-reduce.18 = bf16[768,768]{1,0:T(8,128)(2,1)} all-reduce(f32[768,768]{1,0:T(8,128)} %all-reduce.17.cloned.1.call-done), channel_id=1, replica_groups=mesh['dp'=4,'row'=8,'col'=16] {'col'}, use_global_device_ids=true, to_apply=%region_4.5 | all-reduce | flops 589824 | bytes 3538944 | tf_op jit(solution)/shard_map/psum | solution.py:14
  400.6 11.4 %fusion.25 = bf16[2,64,12,64]{1,3,2,0:T(8,128)(2,1)} fusion(bf16[2,196,12,64]{1,3,2,0:T(8,128)(2,1)S(1)} %copy.80, f32[2,12,64,196]{3,2,1,0:T(8,128)} %fusion.68, f32[2,12,64,196]{3,2,1,0:T(8,128)} %get-tuple-element.127, f32[2,12,64]{2,1,0:T(8,128)S(1)} %broadcast_divide_fusion), kind=kOutput, calls=%fused_computation.21 | convolution fusion | flops 40742596 | bytes 3213312 | tf_op jit(solution)/shard_map/nhqk,nkhd->nqhd/dot_general | solution.py:49
  412.0 11.8 %fusion.12 = f32[2,196,12,64]{1,3,2,0:T(8,128)} fusion(bf16[2,64,12,64]{1,3,2,0:T(8,128)(2,1)S(1)} %copy-done.8, f32[2,12,64,196]{3,2,1,0:T(8,128)} %fusion.68, f32[2,12,64,196]{3,2,1,0:T(8,128)} %get-tuple-element.127, f32[2,12,64]{2,1,0:T(8,128)S(1)} %broadcast_divide_fusion), kind=kOutput, calls=%fused_computation.9 | convolution fusion | flops 40644292 | bytes 3815424 | tf_op jit(solution)/shard_map/nhqk,nqhd->nkhd/dot_general | solution.py:49
  423.9 3.5 copy.84
  434.2 5.9 %convolution_bitcast_fusion = f32[2,196,12,64]{1,3,2,0:T(8,128)} fusion(bf16[2,64,12,64]{1,3,2,0:T(8,128)(2,1)S(1)} %copy-done.2, f32[2,12,64]{2,1,0:T(8,128)S(1)} %broadcast_divide_fusion, f32[2,12,64,196]{3,2,1,0:T(8,128)} %bitcast_select_fusion), kind=kOutput, calls=%fused_computation.11 | convolution fusion | flops 39440068 | bytes 2611200 | tf_op jit(solution)/shard_map/nhqk,nqhd->nkhd/dot_general | solution.py:49
  440.0 3.5 copy.87
  451.3 10.1 %collective-permute-start.12 = (bf16[3,22,768]{2,1,0:T(8,128)(2,1)S(1)}, bf16[3,22,768]{2,1,0:T(8,128)(2,1)S(1)}, u32[]{:S(2)}, u32[]{:S(2)}) collective-permute-start(bf16[3,22,768]{2,1,0:T(8,128)(2,1)S(1)} %get-tuple-element.103), channel_id=1, source_target_pairs={{0,16},{16,32},{32,48},{48,64},{64,80},{80,96},{96,112},{1,17},{17... | collective-permute-start | bytes 304136 | tf_op jit(solution)/shard_map/ppermute | solution.py:24
  463.6 3.6 collective-permute-start.16
  469.4 3.9 collective-permute-done.17
  473.5 9.9 %collective-permute-start.14 = (bf16[8,3,768]{2,1,0:T(4,128)(2,1)S(1)}, bf16[8,3,768]{2,1,0:T(4,128)(2,1)S(1)}, u32[]{:S(2)}, u32[]{:S(2)}) collective-permute-start(bf16[8,3,768]{2,1,0:T(4,128)(2,1)S(1)} %get-tuple-element.115), channel_id=1, source_target_pairs={{0,1},{1,2},{2,3},{3,4},{4,5},{5,6},{6,7},{7,8},{8,9},{9,10},{10,1... | collective-permute-start | bytes 110600 | tf_op jit(solution)/shard_map/ppermute | solution.py:24
  485.4 9.4 %collective-permute-start.18 = (bf16[8,3,768]{2,1,0:T(4,128)(2,1)S(1)}, bf16[8,3,768]{2,1,0:T(4,128)(2,1)S(1)}, u32[]{:S(2)}, u32[]{:S(2)}) collective-permute-start(bf16[8,3,768]{2,1,0:T(4,128)(2,1)S(1)} %get-tuple-element.113), channel_id=1, source_target_pairs={{0,1},{1,2},{2,3},{3,4},{4,5},{5,6},{6,7},{7,8},{8,9},{9,10},{10,1... | collective-permute-start | bytes 110600 | tf_op jit(solution)/shard_map/ppermute | solution.py:24
  497.9 8.0 %collective-permute-done.19 = bf16[8,3,768]{2,1,0:T(4,128)(2,1)S(1)} collective-permute-done((bf16[8,3,768]{2,1,0:T(4,128)(2,1)S(1)}, bf16[8,3,768]{2,1,0:T(4,128)(2,1)S(1)}, u32[]{:S(2)}, u32[]{:S(2)}) %collective-permute-start.19) | collective-permute-done | bytes 36896 | tf_op jit(solution)/shard_map/ppermute | solution.py:24
  (181 shorter events, 58.5 us)
Async XLA Ops:
  8.0 166.1 %all-reduce.17.cloned.1.call-start = ((), (), s32[]{:S(2)}) async-start(), calls=%async_computation.2 | async-start | bytes 4718592 | tf_op jit(solution)/shard_map/psum | solution.py:14
  9.1 32.6 %collective-permute-start.1 = (bf16[3,16,768]{2,1,0:T(8,128)(2,1)S(1)}, bf16[3,16,768]{2,1,0:T(8,128)(2,1)S(1)}, u32[]{:S(2)}, u32[]{:S(2)}) collective-permute-start(bf16[3,16,768]{2,1,0:T(8,128)(2,1)S(1)} %get-tuple-element.119), channel_id=1, source_target_pairs={{16,0},{32,16},{48,32},{64,48},{80,64},{96,80},{112,96},{17,1},{33... | collective-permute-start | bytes 221192 | tf_op jit(solution)/shard_map/ppermute | solution.py:41
  11.8 29.9 %collective-permute-start = (bf16[3,16,768]{2,1,0:T(8,128)(2,1)S(1)}, bf16[3,16,768]{2,1,0:T(8,128)(2,1)S(1)}, u32[]{:S(2)}, u32[]{:S(2)}) collective-permute-start(bf16[3,16,768]{2,1,0:T(8,128)(2,1)S(1)} %get-tuple-element.118), channel_id=1, source_target_pairs={{0,16},{16,32},{32,48},{48,64},{64,80},{80,96},{96,112},{1,17},{17... | collective-permute-start | bytes 221192 | tf_op jit(solution)/shard_map/ppermute | solution.py:39
  15.9 37.2 %collective-permute-start.9 = (bf16[3,16,768]{2,1,0:T(8,128)(2,1)S(1)}, bf16[3,16,768]{2,1,0:T(8,128)(2,1)S(1)}, u32[]{:S(2)}, u32[]{:S(2)}) collective-permute-start(bf16[3,16,768]{2,1,0:T(8,128)(2,1)S(1)} %get-tuple-element.117), channel_id=1, source_target_pairs={{16,0},{32,16},{48,32},{64,48},{80,64},{96,80},{112,96},{17,1},{33... | collective-permute-start | bytes 221192 | tf_op jit(solution)/shard_map/ppermute | solution.py:41
  18.7 8.0 %collective-permute-start.5 = (bf16[3,16]{1,0:T(4,128)(2,1)S(1)}, bf16[3,16]{1,0:T(4,128)(2,1)S(1)}, u32[]{:S(2)}, u32[]{:S(2)}) collective-permute-start(bf16[3,16]{1,0:T(4,128)(2,1)S(1)} %get-tuple-element.125), channel_id=1, source_target_pairs={{16,0},{32,16},{48,32},{64,48},{80,64},{96,80},{112,96},{17,1},{33... | collective-permute-start | bytes 296 | tf_op jit(solution)/shard_map/ppermute | solution.py:41
  21.2 5.5 %collective-permute-start.4 = (bf16[3,16]{1,0:T(4,128)(2,1)S(1)}, bf16[3,16]{1,0:T(4,128)(2,1)S(1)}, u32[]{:S(2)}, u32[]{:S(2)}) collective-permute-start(bf16[3,16]{1,0:T(4,128)(2,1)S(1)} %get-tuple-element.124), channel_id=1, source_target_pairs={{0,16},{16,32},{32,48},{48,64},{64,80},{80,96},{96,112},{1,17},{17... | collective-permute-start | bytes 296 | tf_op jit(solution)/shard_map/ppermute | solution.py:39
  26.8 11.3 %collective-permute-start.7 = (bf16[14,3]{1,0:T(8,128)(2,1)S(1)}, bf16[14,3]{1,0:T(8,128)(2,1)S(1)}, u32[]{:S(2)}, u32[]{:S(2)}) collective-permute-start(bf16[14,3]{1,0:T(8,128)(2,1)S(1)} %get-tuple-element.123), channel_id=1, source_target_pairs={{1,0},{2,1},{3,2},{4,3},{5,4},{6,5},{7,6},{8,7},{9,8},{10,9},{11,1... | collective-permute-start | bytes 260 | tf_op jit(solution)/shard_map/ppermute | solution.py:41
  29.3 11.9 %collective-permute-start.6 = (bf16[14,3]{1,0:T(8,128)(2,1)S(1)}, bf16[14,3]{1,0:T(8,128)(2,1)S(1)}, u32[]{:S(2)}, u32[]{:S(2)}) collective-permute-start(bf16[14,3]{1,0:T(8,128)(2,1)S(1)} %get-tuple-element.122), channel_id=1, source_target_pairs={{0,1},{1,2},{2,3},{3,4},{4,5},{5,6},{6,7},{7,8},{8,9},{9,10},{10,1... | collective-permute-start | bytes 260 | tf_op jit(solution)/shard_map/ppermute | solution.py:39
  38.2 15.0 %collective-permute-start.8 = (bf16[3,16,768]{2,1,0:T(8,128)(2,1)S(1)}, bf16[3,16,768]{2,1,0:T(8,128)(2,1)S(1)}, u32[]{:S(2)}, u32[]{:S(2)}) collective-permute-start(bf16[3,16,768]{2,1,0:T(8,128)(2,1)S(1)} %get-tuple-element.116), channel_id=1, source_target_pairs={{0,16},{16,32},{32,48},{48,64},{64,80},{80,96},{96,112},{1,17},{17... | collective-permute-start | bytes 221192 | tf_op jit(solution)/shard_map/ppermute | solution.py:39
  41.8 22.7 %collective-permute-start.3 = (bf16[14,3,768]{2,1,0:T(4,128)(2,1)S(1)}, bf16[14,3,768]{2,1,0:T(4,128)(2,1)S(1)}, u32[]{:S(2)}, u32[]{:S(2)}) collective-permute-start(bf16[14,3,768]{2,1,0:T(4,128)(2,1)S(1)} %get-tuple-element.111), channel_id=1, source_target_pairs={{1,0},{2,1},{3,2},{4,3},{5,4},{6,5},{7,6},{8,7},{9,8},{10,9},{11,1... | collective-permute-start | bytes 193544 | tf_op jit(solution)/shard_map/ppermute | solution.py:41
  43.7 20.8 %collective-permute-start.2 = (bf16[14,3,768]{2,1,0:T(4,128)(2,1)S(1)}, bf16[14,3,768]{2,1,0:T(4,128)(2,1)S(1)}, u32[]{:S(2)}, u32[]{:S(2)}) collective-permute-start(bf16[14,3,768]{2,1,0:T(4,128)(2,1)S(1)} %get-tuple-element.110), channel_id=1, source_target_pairs={{0,1},{1,2},{2,3},{3,4},{4,5},{5,6},{6,7},{7,8},{8,9},{9,10},{10,1... | collective-permute-start | bytes 193544 | tf_op jit(solution)/shard_map/ppermute | solution.py:39
  53.2 18.0 %collective-permute-start.11 = (bf16[14,3,768]{2,1,0:T(4,128)(2,1)S(1)}, bf16[14,3,768]{2,1,0:T(4,128)(2,1)S(1)}, u32[]{:S(2)}, u32[]{:S(2)}) collective-permute-start(bf16[14,3,768]{2,1,0:T(4,128)(2,1)S(1)} %get-tuple-element.109), channel_id=1, source_target_pairs={{1,0},{2,1},{3,2},{4,3},{5,4},{6,5},{7,6},{8,7},{9,8},{10,9},{11,1... | collective-permute-start | bytes 193544 | tf_op jit(solution)/shard_map/ppermute | solution.py:41
  55.2 16.0 %collective-permute-start.10 = (bf16[14,3,768]{2,1,0:T(4,128)(2,1)S(1)}, bf16[14,3,768]{2,1,0:T(4,128)(2,1)S(1)}, u32[]{:S(2)}, u32[]{:S(2)}) collective-permute-start(bf16[14,3,768]{2,1,0:T(4,128)(2,1)S(1)} %get-tuple-element.108), channel_id=1, source_target_pairs={{0,1},{1,2},{2,3},{3,4},{4,5},{5,6},{6,7},{7,8},{8,9},{9,10},{10,1... | collective-permute-start | bytes 193544 | tf_op jit(solution)/shard_map/ppermute | solution.py:39
  90.0 306.3 %all-gather.2.cloned.1.call-start = ((), (), s32[]{:S(2)}) async-start(), calls=%async_computation.1 | async-start | bytes 1474560 | tf_op jit(solution)/shard_map/all_gather | solution.py:238
  90.6 417.0 %reduce-scatter.2.cloned.1.call-start = ((), (), s32[]{:S(2)}) async-start(), calls=%async_computation.3 | async-start | bytes 1474560 | tf_op jit(solution)/shard_map/reduce_scatter | solution.py:254
  90.7 305.6 %copy-start.13 = (bf16[1,8,16,768]{3,2,1,0:T(8,128)(2,1)S(1)}, bf16[1,8,16,768]{3,2,1,0:T(8,128)(2,1)}, u32[]{:S(2)}) copy-start(bf16[1,8,16,768]{3,2,1,0:T(8,128)(2,1)} %param.27) | copy-start | bytes 589828
  451.3 17.9 %collective-permute-start.12 = (bf16[3,22,768]{2,1,0:T(8,128)(2,1)S(1)}, bf16[3,22,768]{2,1,0:T(8,128)(2,1)S(1)}, u32[]{:S(2)}, u32[]{:S(2)}) collective-permute-start(bf16[3,22,768]{2,1,0:T(8,128)(2,1)S(1)} %get-tuple-element.103), channel_id=1, source_target_pairs={{0,16},{16,32},{32,48},{48,64},{64,80},{80,96},{96,112},{1,17},{17... | collective-permute-start | bytes 304136 | tf_op jit(solution)/shard_map/ppermute | solution.py:24
  461.6 7.6 %collective-permute-start.13 = (bf16[3,22,768]{2,1,0:T(8,128)(2,1)S(1)}, bf16[3,22,768]{2,1,0:T(8,128)(2,1)S(1)}, u32[]{:S(2)}, u32[]{:S(2)}) collective-permute-start(bf16[3,22,768]{2,1,0:T(8,128)(2,1)S(1)} %get-tuple-element.102), channel_id=1, source_target_pairs={{16,0},{32,16},{48,32},{64,48},{80,64},{96,80},{112,96},{17,1},{33... | collective-permute-start | bytes 304136 | tf_op jit(solution)/shard_map/ppermute | solution.py:24
  463.6 5.7 %collective-permute-start.16 = (bf16[3,22,768]{2,1,0:T(8,128)(2,1)S(1)}, bf16[3,22,768]{2,1,0:T(8,128)(2,1)S(1)}, u32[]{:S(2)}, u32[]{:S(2)}) collective-permute-start(bf16[3,22,768]{2,1,0:T(8,128)(2,1)S(1)} %get-tuple-element.101), channel_id=1, source_target_pairs={{0,16},{16,32},{32,48},{48,64},{64,80},{80,96},{96,112},{1,17},{17... | collective-permute-start | bytes 304136 | tf_op jit(solution)/shard_map/ppermute | solution.py:24
  467.3 6.1 %collective-permute-start.17 = (bf16[3,22,768]{2,1,0:T(8,128)(2,1)S(1)}, bf16[3,22,768]{2,1,0:T(8,128)(2,1)S(1)}, u32[]{:S(2)}, u32[]{:S(2)}) collective-permute-start(bf16[3,22,768]{2,1,0:T(8,128)(2,1)S(1)} %get-tuple-element.100), channel_id=1, source_target_pairs={{16,0},{32,16},{48,32},{64,48},{80,64},{96,80},{112,96},{17,1},{33... | collective-permute-start | bytes 304136 | tf_op jit(solution)/shard_map/ppermute | solution.py:24
  473.5 23.2 %collective-permute-start.14 = (bf16[8,3,768]{2,1,0:T(4,128)(2,1)S(1)}, bf16[8,3,768]{2,1,0:T(4,128)(2,1)S(1)}, u32[]{:S(2)}, u32[]{:S(2)}) collective-permute-start(bf16[8,3,768]{2,1,0:T(4,128)(2,1)S(1)} %get-tuple-element.115), channel_id=1, source_target_pairs={{0,1},{1,2},{2,3},{3,4},{4,5},{5,6},{6,7},{7,8},{8,9},{9,10},{10,1... | collective-permute-start | bytes 110600 | tf_op jit(solution)/shard_map/ppermute | solution.py:24
  483.4 13.8 %collective-permute-start.15 = (bf16[8,3,768]{2,1,0:T(4,128)(2,1)S(1)}, bf16[8,3,768]{2,1,0:T(4,128)(2,1)S(1)}, u32[]{:S(2)}, u32[]{:S(2)}) collective-permute-start(bf16[8,3,768]{2,1,0:T(4,128)(2,1)S(1)} %get-tuple-element.114), channel_id=1, source_target_pairs={{1,0},{2,1},{3,2},{4,3},{5,4},{6,5},{7,6},{8,7},{9,8},{10,9},{11,1... | collective-permute-start | bytes 110600 | tf_op jit(solution)/shard_map/ppermute | solution.py:24
  485.4 11.4 %collective-permute-start.18 = (bf16[8,3,768]{2,1,0:T(4,128)(2,1)S(1)}, bf16[8,3,768]{2,1,0:T(4,128)(2,1)S(1)}, u32[]{:S(2)}, u32[]{:S(2)}) collective-permute-start(bf16[8,3,768]{2,1,0:T(4,128)(2,1)S(1)} %get-tuple-element.113), channel_id=1, source_target_pairs={{0,1},{1,2},{2,3},{3,4},{4,5},{5,6},{6,7},{7,8},{8,9},{9,10},{10,1... | collective-permute-start | bytes 110600 | tf_op jit(solution)/shard_map/ppermute | solution.py:24
  494.8 11.1 %collective-permute-start.19 = (bf16[8,3,768]{2,1,0:T(4,128)(2,1)S(1)}, bf16[8,3,768]{2,1,0:T(4,128)(2,1)S(1)}, u32[]{:S(2)}, u32[]{:S(2)}) collective-permute-start(bf16[8,3,768]{2,1,0:T(4,128)(2,1)S(1)} %get-tuple-element.112), channel_id=1, source_target_pairs={{1,0},{2,1},{3,2},{4,3},{5,4},{6,5},{7,6},{8,7},{9,8},{10,9},{11,1... | collective-permute-start | bytes 110600 | tf_op jit(solution)/shard_map/ppermute | solution.py:24
  (18 other events, 198.7 us)
Sparse Core Ops, SparseCore 0:
  90.1 83.9 all-reduce.16
Sparse Core Ops, SparseCore 1:
  92.6 43.1 all-gather.1
  396.4 45.5 reduce-scatter.1
